TPU v7x, 128 devices: a whole 4x4x4 slice. The times are simulated.
128 devices in a mesh: row: 8 (over z_lo, y), col: 16 (over z_hi, x, core).
Axes of the slice: x: 4, y: 4, z: 4 (z_hi: 2, z_lo: 2; z = z_hi * 2 + z_lo), core: 2. Of those that a mesh axis runs over, the one named last changes fastest.
Arguments:
- observed: float32 [4, 65536], P(None, ('row', 'col')), may hold values from -50 to 50
- tile_values: bfloat16 [256, 32, 256, 256], P('row', 'col'), may hold values from -2.2649514 to 2.2649514
- tile_cols: int32 [256, 32], P('row', 'col'), may hold values from 0 to 255
Outputs:
- solution: float32 [4, 1048576], P(None, ('col', 'row'))
- residual_ratio: float32 [4], replicated
All inputs are finite; a program needn't handle non-finite values.
Results may differ from a plain program's by a relative error of at most 0.0021.
Values may be sent and summed in bfloat16 or wider, within the bound.
A program may use at most 128 MiB of HBM per device.

v0:
```python
import jax
import jax.numpy as jnp
from jax import lax
from jax.sharding import PartitionSpec as P

ITERS = 2
N = 1048576
epsilon_sq = 1e-06


def local(observed, tile_values, tile_cols):
    right_sides = observed.shape[0]
    row_tiles = tile_values.shape[0]
    per_block = tile_values.shape[1]
    tile_size = tile_values.shape[2]
    col_tiles = N // (tile_size * lax.axis_size("col"))
    panel_len = col_tiles * tile_size
    share_len = panel_len // lax.axis_size("row")
    flat_cols = tile_cols.reshape(-1)

    def adjoint_map(left_bf):
        gathered = lax.all_gather(left_bf, "col", axis=1, tiled=True).reshape(
            right_sides, row_tiles, tile_size
        )
        tile_terms = jnp.einsum(
            "rktj,nrt->nrkj", tile_values, gathered, preferred_element_type=jnp.float32
        )
        tile_terms = tile_terms.reshape(right_sides, row_tiles * per_block, tile_size)
        placed = (
            jnp.zeros((right_sides, col_tiles, tile_size), jnp.float32)
            .at[:, flat_cols]
            .add(tile_terms)
        )
        placed = placed.reshape(right_sides, panel_len)
        summed = lax.psum_scatter(placed, "row", scatter_dimension=1, tiled=True)
        return summed

    def lanczos_pair(left_raw, right_vec):
        beta_sq = lax.psum(jnp.sum(left_raw * left_raw, axis=1), ("row", "col"))
        beta_norm = jnp.sqrt(beta_sq + epsilon_sq)
        product = adjoint_map(left_raw.astype(jnp.bfloat16))
        right_raw = product / beta_norm[:, None] - beta_norm[:, None] * right_vec
        alpha_sq = lax.psum(jnp.sum(right_raw * right_raw, axis=1), ("row", "col"))
        alpha_norm = jnp.sqrt(alpha_sq + epsilon_sq)
        return (beta_norm, alpha_norm, right_raw)

    blank_right = jnp.zeros((right_sides, share_len), jnp.float32)
    beta_norm, alpha_norm, right_raw = lanczos_pair(observed, blank_right)
    first_beta = beta_norm
    left_vec = observed / beta_norm[:, None]
    right_vec = right_raw / alpha_norm[:, None]
    right_bf = right_raw.astype(jnp.bfloat16)
    phibar = beta_norm
    rhobar = alpha_norm
    direction = right_vec
    solution = jnp.zeros_like(right_vec)
    for iteration in range(ITERS):
        whole_panel = lax.all_gather(right_bf, "row", axis=1, tiled=True)
        picked = jnp.take(whole_panel.reshape(right_sides, col_tiles, tile_size), tile_cols, axis=1)
        partial_rows = jnp.einsum(
            "rktj,nrkj->nrt", tile_values, picked, preferred_element_type=jnp.float32
        )
        left_raw = (
            lax.psum_scatter(
                partial_rows.reshape(right_sides, row_tiles * tile_size),
                "col",
                scatter_dimension=1,
                tiled=True,
            )
            / alpha_norm[:, None]
            - alpha_norm[:, None] * left_vec
        )
        beta_norm, alpha_norm, right_raw = lanczos_pair(left_raw, right_vec)
        left_vec = left_raw / beta_norm[:, None]
        right_vec = right_raw / alpha_norm[:, None]
        right_bf = right_raw.astype(jnp.bfloat16)
        rho_val = jnp.sqrt(rhobar * rhobar + beta_norm * beta_norm)
        cosine = rhobar / rho_val
        sine_val = beta_norm / rho_val
        theta_val = sine_val * alpha_norm
        rhobar = -cosine * alpha_norm
        phi_val = cosine * phibar
        phibar = sine_val * phibar
        solution = solution + (phi_val / rho_val)[:, None] * direction
        direction = right_vec - (theta_val / rho_val)[:, None] * direction
    return (solution, phibar / first_beta)


def solution(mesh):
    in_specs = (P(None, ("row", "col")), P("row", "col", None, None), P("row", "col"))
    out_specs = (P(None, ("col", "row")), P())
    return jax.shard_map(local, mesh=mesh, in_specs=in_specs, out_specs=out_specs, check_vma=False)
```

profile of v0, /device:TPU:1, one launch (start us, length us, event | category | flops | bytes accessed | tf_op | source)
XLA Modules:
  0.0 1160.2 jit_solution(9524676217768432283)
XLA Ops:
  8.1 26.5 %all_gather.12 = bf16[4,8192]{1,0:T(4,128)(2,1)S(1)} all-gather(bf16[4,512]{1,0:T(4,128)(2,1)S(1)} %get-tuple-element.13), channel_id=1, replica_groups=mesh['row'=8,'col'=16] {'col'}, dimensions={1}, use_global_device_ids=true | all-gather | bytes 69632 | tf_op jit(solution)/shard_map/all_gather | solution.py:22
  35.5 4.6 fusion.21
  40.2 2.8 scatter_fusion
  43.0 16.1 %copy.26 = f32[4,65536]{0,1:T(8,128)} copy(f32[4,65536]{1,0:T(4,128)S(1)} %bitcast.65) | data formatting | bytes 2097152
  59.2 369.9 %psum.35 = f32[4]{0:T(128)S(1)} all-reduce(f32[4]{0:T(128)S(1)} %get-tuple-element.14), channel_id=1, replica_groups=mesh['row'=8,'col'=16] {'row','col'}, use_global_device_ids=true, to_apply=%region_3.0 | all-reduce | flops 4 | bytes 32 | tf_op jit(solution)/shard_map/psum | solution.py:39
  429.5 2.8 copy.27
  432.6 22.8 %all_gather.13 = bf16[4,65536]{1,0:T(4,128)(2,1)S(1)} all-gather(bf16[4,8192]{1,0:T(4,128)(2,1)S(1)} %convert_element_type.13), channel_id=1, replica_groups=mesh['row'=8,'col'=16] {'row'}, dimensions={1}, use_global_device_ids=true | all-gather | bytes 589824 | tf_op jit(solution)/shard_map/all_gather | solution.py:58
  456.1 5.7 fusion.2
  461.8 2.6 copy.28
  464.5 74.8 %psum.36 = f32[4]{0:T(128)S(1)} all-reduce(f32[4]{0:T(128)S(1)} %get-tuple-element.11), channel_id=1, replica_groups=mesh['row'=8,'col'=16] {'row','col'}, use_global_device_ids=true, to_apply=%region_5.0 | all-reduce | flops 4 | bytes 32 | tf_op jit(solution)/shard_map/psum | solution.py:43
  539.4 8.0 reduce-scatter.15.cloned.1.call-done
  547.4 1.1 copy.29
  548.7 23.2 %all_gather.14 = bf16[4,8192]{1,0:T(4,128)(2,1)S(1)} all-gather(bf16[4,512]{1,0:T(4,128)(2,1)S(1)} %convert_element_type.14), channel_id=1, replica_groups=mesh['row'=8,'col'=16] {'col'}, dimensions={1}, use_global_device_ids=true | all-gather | bytes 69632 | tf_op jit(solution)/shard_map/all_gather | solution.py:22
  571.8 4.6 fusion.22
  576.6 2.8 scatter_fusion.1
  579.4 16.1 %copy.30 = f32[4,65536]{0,1:T(8,128)} copy(f32[4,65536]{1,0:T(4,128)S(1)} %bitcast.64) | data formatting | bytes 2097152
  595.6 371.7 %psum.37 = f32[4]{0:T(128)S(1)} all-reduce(f32[4]{0:T(128)S(1)} %get-tuple-element.9), channel_id=1, replica_groups=mesh['row'=8,'col'=16] {'row','col'}, use_global_device_ids=true, to_apply=%region_8.10 | all-reduce | flops 4 | bytes 32 | tf_op jit(solution)/shard_map/psum | solution.py:39
  967.3 2.8 copy.31
  970.3 23.0 %all_gather.15 = bf16[4,65536]{1,0:T(4,128)(2,1)S(1)} all-gather(bf16[4,8192]{1,0:T(4,128)(2,1)S(1)} %get-tuple-element.7), channel_id=1, replica_groups=mesh['row'=8,'col'=16] {'row'}, dimensions={1}, use_global_device_ids=true | all-gather | bytes 589824 | tf_op jit(solution)/shard_map/all_gather | solution.py:58
  994.0 5.7 fusion
  999.7 2.6 copy.32
  1002.5 75.0 %psum.38 = f32[4]{0:T(128)S(1)} all-reduce(f32[4]{0:T(128)S(1)} %multiply_reduce_fusion), channel_id=1, replica_groups=mesh['row'=8,'col'=16] {'row','col'}, use_global_device_ids=true, to_apply=%region_12.14 | all-reduce | flops 4 | bytes 32 | tf_op jit(solution)/shard_map/psum | solution.py:43
  1077.5 8.0 reduce-scatter.19.cloned.1.call-done
  1086.7 65.6 %psum.39 = f32[4]{0:T(128)S(1)} all-reduce(f32[4]{0:T(128)S(1)} %fusion.11), channel_id=1, replica_groups=mesh['row'=8,'col'=16] {'row','col'}, use_global_device_ids=true, to_apply=%region_15.17 | all-reduce | flops 4 | bytes 32 | tf_op jit(solution)/shard_map/psum | solution.py:39
  (43 shorter events, 7.5 us)
Async XLA Ops:
  7.2 422.3 %reduce-scatter.13.cloned.1.call-start = ((), (), s32[]{:S(2)}) async-start(), calls=%async_computation.4 | async-start | bytes 37748736
  59.1 370.0 %copy-start.1 = (s32[32,2]{0,1:T(2,128)S(1)}, s32[32,2]{0,1:T(2,128)}, u32[]{:S(2)}) copy-start(s32[32,2]{0,1:T(2,128)} %param.7) | copy-start | bytes 772
  59.1 488.2 %reduce-scatter.15.cloned.1.call-start = ((), (), s32[]{:S(2)}) async-start(), calls=%async_computation.5 | async-start | bytes 4456448
  456.1 92.3 %copy-start = (f32[4,512]{1,0:T(4,128)S(1)}, f32[4,512]{1,0:T(4,128)}, u32[]{:S(2)}) copy-start(f32[4,512]{1,0:T(4,128)} %param.5) | copy-start | bytes 24580
  464.5 502.9 %reduce-scatter.17.cloned.1.call-start = ((), (), s32[]{:S(2)}) async-start(), calls=%async_computation.6 | async-start | bytes 37748736
  595.5 490.0 %reduce-scatter.19.cloned.1.call-start = ((), (), s32[]{:S(2)}) async-start(), calls=%async_computation.7 | async-start | bytes 4456448
Sparse Core Ops, SparseCore 0:
  59.3 325.6 reduce-scatter.12
  464.6 82.7 reduce-scatter.14
  595.6 327.5 reduce-scatter.16
  1002.6 82.7 reduce-scatter.18
where the time goes:
time: 1160 us
  blocking collectives  1050 us (91%)
  local copies, waits for them, and re-layouts  48 us (4%)
  matrix products  20.5 us (2%)
  waiting for transfers between devices  16.1 us (1%)
  between operations  13.9 us (1%)
    psum x3, blocking collectives, lanczos_pair(): beta_sq = lax.psum(jnp.sum(left_raw * left_raw, axis=1), ('row', 'col'))  807 us
    psum x2, blocking collectives, lanczos_pair(): alpha_sq = lax.psum(jnp.sum(right_raw * right_raw, axis=1), ('row', 'col'))  150 us
    all_gather x2, blocking collectives, adjoint_map(): lax.all_gather(left_bf, 'col', axis=1, tiled=True)  49.7 us
    unnamed x13, local copies, waits for them, and re-layouts  46 us
    all_gather x2, blocking collectives, local(): whole_panel = lax.all_gather(right_bf, 'row', axis=1, tiled=True)  45.8 us
  transfers between devices with their start and end apart: 4, of which 2 were waited for; matrix products, arithmetic and copies ran while one was open for 0% of the time, Pallas kernels for 0%

commit v1 on v0

--- a/solution.py
+++ b/solution.py
@@ -36,7 +36,9 @@
         return summed
 
     def lanczos_pair(left_raw, right_vec):
-        beta_sq = lax.psum(jnp.sum(left_raw * left_raw, axis=1), ("row", "col"))
+        beta_sq = jax.lax.all_gather(jnp.sum(left_raw * left_raw, axis=1), ("row", "col")).sum(
+            axis=0
+        )
         beta_norm = jnp.sqrt(beta_sq + epsilon_sq)
         product = adjoint_map(left_raw.astype(jnp.bfloat16))
         right_raw = product / beta_norm[:, None] - beta_norm[:, None] * right_vec

time: 1160 us -> 1230 us (1.060)
  waiting for transfers between devices: 16.1 us -> 90.6 us
    unnamed x0 -> x3, blocking collectives: none -> 809 us
    psum x3 -> x0, blocking collectives: 807 us -> none  [lanczos_pair(): beta_sq = lax.psum(jnp.sum(left_raw * left_raw, axis=1), ('row', 'col'))]
    unnamed x8, waiting for transfers between devices: 16.1 us -> 90.6 us
    psum x2, blocking collectives: 150 us -> 138 us  [lanczos_pair(): alpha_sq = lax.psum(jnp.sum(right_raw * right_raw, axis=1), ('row', 'col'))]
    unnamed x13 -> x19, local copies, waits for them, and re-layouts: 46 us -> 46.7 us
where the time goes in v1:
time: 1230 us
  blocking collectives  1040 us (85%)
  waiting for transfers between devices  90.6 us (7%)
  local copies, waits for them, and re-layouts  49.1 us (4%)
  matrix products  20.5 us (2%)
  between operations  14 us (1%)
    unnamed x3, blocking collectives  809 us
    psum x2, blocking collectives, lanczos_pair(): alpha_sq = lax.psum(jnp.sum(right_raw * right_raw, axis=1), ('row', 'col'))  138 us
    unnamed x8, waiting for transfers between devices  90.6 us
    all_gather x2, blocking collectives, adjoint_map(): lax.all_gather(left_bf, 'col', axis=1, tiled=True)  49.6 us
    unnamed x19, local copies, waits for them, and re-layouts  46.7 us
    all_gather x2, blocking collectives, local(): whole_panel = lax.all_gather(right_bf, 'row', axis=1, tiled=True)  45.7 us
  transfers between devices with their start and end apart: 4, of which 2 were waited for; matrix products, arithmetic and copies ran while one was open for 0% of the time, Pallas kernels for 0%

profile of v1, /device:TPU:1, one launch (start us, length us, event | category | flops | bytes accessed | tf_op | source)
XLA Modules:
  0.0 1225.1 jit_solution(4320062039801442796)
XLA Ops:
  9.0 26.5 %all_gather.30 = bf16[4,8192]{1,0:T(4,128)(2,1)S(1)} all-gather(bf16[4,512]{1,0:T(4,128)(2,1)S(1)} %get-tuple-element.13), channel_id=1, replica_groups=mesh['row'=8,'col'=16] {'col'}, dimensions={1}, use_global_device_ids=true | all-gather | bytes 69632 | tf_op jit(solution)/shard_map/all_gather | solution.py:22
  35.5 4.6 fusion.21
  40.2 2.8 scatter_fusion
  43.1 16.1 %copy.26 = f32[4,65536]{0,1:T(8,128)} copy(f32[4,65536]{1,0:T(4,128)S(1)} %bitcast.65) | data formatting | bytes 2097152
  59.5 371.6 %all-reduce = f32[512]{0:T(512)S(1)} all-reduce(f32[512]{0:T(512)S(1)} %dynamic-update-slice), channel_id=2, replica_groups=mesh['row'=8,'col'=16] {'row','col'}, use_global_device_ids=true, to_apply=%add | all-reduce | flops 512 | bytes 4096
  431.6 2.8 copy.27
  434.7 62.5 %psum.14 = f32[4]{0:T(128)S(1)} all-reduce(f32[4]{0:T(128)S(1)} %get-tuple-element.11), channel_id=1, replica_groups=mesh['row'=8,'col'=16] {'row','col'}, use_global_device_ids=true, to_apply=%region_5.0 | all-reduce | flops 4 | bytes 32 | tf_op jit(solution)/shard_map/psum | solution.py:45
  497.3 22.9 %all_gather.33 = bf16[4,65536]{1,0:T(4,128)(2,1)S(1)} all-gather(bf16[4,8192]{1,0:T(4,128)(2,1)S(1)} %convert_element_type.13), channel_id=1, replica_groups=mesh['row'=8,'col'=16] {'row'}, dimensions={1}, use_global_device_ids=true | all-gather | bytes 589824 | tf_op jit(solution)/shard_map/all_gather | solution.py:60
  520.9 5.7 fusion.2
  526.5 2.6 copy.28
  529.2 82.5 %reduce-scatter.15.cloned.1.call-done = f32[512,4]{1,0:T(8,128)} async-done(((f32[8192,4]{1,0:T(8,128)}), f32[512,4]{1,0:T(8,128)}) %reduce-scatter.15.cloned.1.call-update) | async-done | bytes 8208
  611.8 1.1 copy.29
  613.0 23.1 %all_gather.36 = bf16[4,8192]{1,0:T(4,128)(2,1)S(1)} all-gather(bf16[4,512]{1,0:T(4,128)(2,1)S(1)} %convert_element_type.14), channel_id=1, replica_groups=mesh['row'=8,'col'=16] {'col'}, dimensions={1}, use_global_device_ids=true | all-gather | bytes 69632 | tf_op jit(solution)/shard_map/all_gather | solution.py:22
  636.2 4.6 fusion.22
  640.9 2.8 scatter_fusion.1
  643.7 16.1 %copy.30 = f32[4,65536]{0,1:T(8,128)} copy(f32[4,65536]{1,0:T(4,128)S(1)} %bitcast.64) | data formatting | bytes 2097152
  660.1 371.8 %all-reduce.1 = f32[512]{0:T(512)S(1)} all-reduce(f32[512]{0:T(512)S(1)} %dynamic-update-slice.1), channel_id=3, replica_groups=mesh['row'=8,'col'=16] {'row','col'}, use_global_device_ids=true, to_apply=%add.1 | all-reduce | flops 512 | bytes 4096
  1032.1 2.8 copy.31
  1035.1 22.8 %all_gather.37 = bf16[4,65536]{1,0:T(4,128)(2,1)S(1)} all-gather(bf16[4,8192]{1,0:T(4,128)(2,1)S(1)} %get-tuple-element.7), channel_id=1, replica_groups=mesh['row'=8,'col'=16] {'row'}, dimensions={1}, use_global_device_ids=true | all-gather | bytes 589824 | tf_op jit(solution)/shard_map/all_gather | solution.py:60
  1058.6 5.7 fusion
  1064.3 2.6 copy.32
  1067.1 75.0 %psum.15 = f32[4]{0:T(128)S(1)} all-reduce(f32[4]{0:T(128)S(1)} %multiply_reduce_fusion), channel_id=1, replica_groups=mesh['row'=8,'col'=16] {'row','col'}, use_global_device_ids=true, to_apply=%region_12.14 | all-reduce | flops 4 | bytes 32 | tf_op jit(solution)/shard_map/psum | solution.py:45
  1142.1 7.9 reduce-scatter.19.cloned.1.call-done
  1151.5 65.5 %all-reduce.2 = f32[512]{0:T(512)S(1)} all-reduce(f32[512]{0:T(512)S(1)} %dynamic-update-slice.2), channel_id=4, replica_groups=mesh['row'=8,'col'=16] {'row','col'}, use_global_device_ids=true, to_apply=%add.2 | all-reduce | flops 512 | bytes 4096
  (55 shorter events, 8.6 us)
Async XLA Ops:
  7.2 424.4 %reduce-scatter.13.cloned.1.call-start = ((), (), s32[]{:S(2)}) async-start(), calls=%async_computation.4 | async-start | bytes 37748736
  59.1 372.1 %copy-start.1 = (s32[32,2]{0,1:T(2,128)S(1)}, s32[32,2]{0,1:T(2,128)}, u32[]{:S(2)}) copy-start(s32[32,2]{0,1:T(2,128)} %param.7) | copy-start | bytes 772
  59.2 552.6 %reduce-scatter.15.cloned.1.call-start = ((), (), s32[]{:S(2)}) async-start(), calls=%async_computation.5 | async-start | bytes 4456448
  520.9 92.0 %copy-start = (f32[4,512]{1,0:T(4,128)S(1)}, f32[4,512]{1,0:T(4,128)}, u32[]{:S(2)}) copy-start(f32[4,512]{1,0:T(4,128)} %param.5) | copy-start | bytes 24580
  529.2 502.9 %reduce-scatter.17.cloned.1.call-start = ((), (), s32[]{:S(2)}) async-start(), calls=%async_computation.6 | async-start | bytes 37748736
  659.8 490.2 %reduce-scatter.19.cloned.1.call-start = ((), (), s32[]{:S(2)}) async-start(), calls=%async_computation.7 | async-start | bytes 4456448
Sparse Core Ops, SparseCore 0:
  59.3 325.7 reduce-scatter.12
  529.3 82.4 reduce-scatter.14
  660.0 327.8 reduce-scatter.16
  1067.2 82.7 reduce-scatter.18
